TPU v7x, 32 devices: a whole 2x2x4 slice. The times are simulated.
32 devices in a mesh: phase: 2 (over x), expert: 4 (over y, core), tensor: 4 (over z).
Axes of the slice: x: 2, y: 2, z: 4, core: 2. Of those that a mesh axis runs over, the one named last changes fastest.
Arguments:
- forward_routes: int32 [2, 256, 6], P('phase', 'expert'), may hold values from 0 to 11, all different within a row; in each aligned block of 64 rows (0 to 63, 64 to 127, ..., all dimensions but the last counted through in order) at most 43 rows name the same one
- forward_gates: float32 [2, 256, 6], P('phase', 'expert'), may hold values from 0.05 to 1
- hidden_rows: bfloat16 [2, 12, 4, 43, 1024], P('phase', 'expert', None, None, 'tensor'), may hold values from -6 to 6
- down_weight: bfloat16 [2, 12, 1024, 2560], P('phase', 'expert', 'tensor'), may hold values from -0.1875 to 0.1875
- shared_hidden: bfloat16 [2, 256, 1536], P('phase', 'expert', 'tensor'), may hold values from -6 to 6
- shared_weight: bfloat16 [2, 1536, 2560], P('phase', 'tensor', 'expert'), may hold values from -0.15625 to 0.15625
- backward_routes: int32 [2, 256, 6], P('phase', 'expert'), may hold values from 0 to 11, all different within a row; in each aligned block of 64 rows (0 to 63, 64 to 127, ..., all dimensions but the last counted through in order) at most 43 rows name the same one
- backward_gates: float32 [2, 256, 6], P('phase', 'expert'), may hold values from 0.05 to 1
- cotangent: bfloat16 [2, 256, 2560], P('phase', 'expert', 'tensor'), may hold values from -6 to 6
Outputs:
- forward_next: bfloat16 [2, 256, 2560], P('phase', 'expert', 'tensor')
- hidden_grad: bfloat16 [2, 12, 4, 43, 1024], P('phase', 'expert', None, None, 'tensor')
- shared_grad: bfloat16 [2, 256, 1536], P('phase', 'expert', 'tensor')
Inputs may be any that keep to these rules, and one draw needn't show every extreme that they name: `forward_routes`: each token names 6 different experts. The tokens of one token group (the 64 rows of one device) name any one expert 43 times at most, and some group reaches that. `backward_routes`: as for forward_routes.
All inputs are finite; a program needn't handle non-finite values.
Results may differ from a plain program's by a relative error of at most 0.0049.
Values may be sent and summed in bfloat16 or wider, within the bound.
A program may use at most 64 MiB of HBM per device.

v0:
```python
import jax
import jax.numpy as jnp
from jax import lax
from jax.sharding import PartitionSpec as P


def shifted(value, axis, steps):
    count = lax.axis_size(axis)
    pairs = [(source, (source + steps) % count) for source in range(count)]
    return lax.ppermute(value, axis, pairs)


def slot_numbers(routes, experts):
    numbers = jnp.arange(experts, dtype=jnp.int32)
    onehot = (routes[:, :, None] == numbers[None, None, :]).astype(jnp.int32)
    per_token = jnp.sum(onehot, axis=1)
    before = jnp.cumsum(per_token, axis=0) - per_token
    return jnp.sum(onehot * before[:, None, :], axis=2)


def row_positions(routes, experts_here, groups, capacity):
    slot_index = slot_numbers(routes, experts_here * groups)
    holder = routes // experts_here
    within = routes - holder * experts_here
    return ((within * groups + holder) * capacity + slot_index).reshape(-1)


def place_rows(gates, values, positions, total_rows):
    scaled = (gates[:, :, None] * values[:, None, :].astype(jnp.float32)).astype(jnp.bfloat16)
    outgoing = jnp.zeros((total_rows, values.shape[1]), jnp.bfloat16)
    return outgoing.at[positions].set(scaled.reshape(-1, values.shape[1]))


def on_device(
    forward_routes,
    forward_gates,
    hidden_rows,
    down_weight,
    shared_hidden,
    shared_weight,
    backward_routes,
    backward_gates,
    cotangent,
):
    experts_here = down_weight.shape[1]
    features = down_weight.shape[3]
    capacity = hidden_rows.shape[3]
    groups = lax.axis_size("expert")
    token_count = forward_routes.shape[1]
    top_count = forward_routes.shape[2]
    hidden = hidden_rows[0]
    weight = down_weight[0]
    local_shared = shared_hidden[0]
    shared_piece = shared_weight[0]
    shared_part = jnp.dot(
        local_shared,
        lax.all_gather(shared_piece, "expert", axis=1, tiled=True),
        preferred_element_type=jnp.float32,
    )
    fore_positions = row_positions(forward_routes[0], experts_here, groups, capacity)
    fore_gates = forward_gates[0]
    partial_value = jnp.einsum(
        "egmh,ehd->egmd", hidden, weight, preferred_element_type=jnp.float32
    ).astype(jnp.bfloat16)
    arrived = lax.all_to_all(partial_value, "expert", split_axis=1, concat_axis=1, tiled=True)
    picked = arrived.reshape(-1, features)[fore_positions].reshape(token_count, top_count, features)
    summand = shared_part + jnp.sum(picked.astype(jnp.float32) * fore_gates[:, :, None], axis=1)
    summed = lax.psum_scatter(summand, "tensor", scatter_dimension=1, tiled=True)
    layer_out = summed.astype(jnp.bfloat16)
    handed = shifted(layer_out, "phase", 1)
    cotangent_whole = lax.all_gather(cotangent[0], "tensor", axis=1, tiled=True)
    back_positions = row_positions(backward_routes[0], experts_here, groups, capacity)
    total_rows = experts_here * groups * capacity
    outgoing = place_rows(backward_gates[0], cotangent_whole, back_positions, total_rows)
    received = lax.all_to_all(
        outgoing.reshape(experts_here, groups, capacity, features),
        "expert",
        split_axis=1,
        concat_axis=1,
        tiled=True,
    )
    hidden_back = jnp.einsum(
        "egmd,ehd->egmh", received, weight, preferred_element_type=jnp.float32
    ).astype(jnp.bfloat16)
    shared_back = lax.dot_general(
        cotangent_whole,
        lax.all_gather(shared_piece, "expert", axis=1, tiled=True),
        (((1,), (1,)), ((), ())),
        preferred_element_type=jnp.float32,
    )
    return (handed[None], hidden_back[None], shared_back.astype(jnp.bfloat16)[None])


def solution(mesh):
    return jax.shard_map(
        on_device,
        mesh=mesh,
        in_specs=(
            P("phase", "expert", None),
            P("phase", "expert", None),
            P("phase", "expert", None, None, "tensor"),
            P("phase", "expert", "tensor", None),
            P("phase", "expert", "tensor"),
            P("phase", "tensor", "expert"),
            P("phase", "expert", None),
            P("phase", "expert", None),
            P("phase", "expert", "tensor"),
        ),
        out_specs=(
            P("phase", "expert", "tensor"),
            P("phase", "expert", None, None, "tensor"),
            P("phase", "expert", "tensor"),
        ),
        check_vma=False,
    )
```

profile of v0, /device:TPU:0, one launch (start us, length us, event | category | flops | bytes accessed | tf_op | source)
XLA Modules:
  0.0 125.8 jit_solution(11114866038983174019)
XLA Ops:
  7.2 0.0 all-gather.4.cloned.1.call-start
  7.2 0.7 all-gather.4.cloned.1.call-update
  7.9 3.2 %convolution_convert_fusion = bf16[3,4,43,2560]{3,2,1,0:T(8,128)(2,1)S(1)} fusion(bf16[1,3,256,2560]{3,2,1,0:T(8,128)(2,1)} %param.12, bf16[3,4,43,256]{3,1,2,0:T(4,128)(2,1)} %bitcast.42), kind=kOutput, calls=%fused_computation.3 | convolution fusion | flops 677652480 | bytes 6838272 | tf_op jit(solution)/shard_map/egmh,ehd->egmd/dot_general | solution.py:62
  11.1 1.8 %copy.38 = bf16[3,4,43,2560]{3,2,0,1:T(8,128)(2,1)} copy(bf16[3,4,43,2560]{3,2,1,0:T(8,128)(2,1)S(1)} %convolution_convert_fusion) | data formatting | bytes 5283840 | tf_op jit(solution)/shard_map/convert_element_type | solution.py:64
  12.8 4.4 %all-to-all-start = ((bf16[3,4,43,2560]{3,2,0,1:T(8,128)(2,1)}), bf16[3,4,43,2560]{3,2,0,1:T(8,128)(2,1)S(1)}, u32[]{:S(2)}, u32[]{:S(2)}) async-start(bf16[3,4,43,2560]{3,2,0,1:T(8,128)(2,1)} %copy.38), calls=%async_computation | async-start | bytes 5898240 | tf_op jit(solution)/shard_map/all_to_all | solution.py:65
  17.2 0.1 copy.46
  17.4 0.1 copy.47
  17.4 0.1 reduce_window_sum.18
  17.5 0.1 copy.49
  17.7 0.1 copy.50
  17.8 0.1 reduce_sum.55
  17.9 0.1 copy.51
  18.0 0.1 mul.123
  18.1 0.1 squeeze.26
  18.3 15.6 %all-gather.1 = bf16[1,64,2560]{2,1,0:T(8,128)(2,1)S(1)} all-gather(bf16[1,64,640]{2,1,0:T(8,128)(2,1)S(1)} %copy-done.2), channel_id=3, replica_groups=mesh['phase'=2,'expert'=4,'tensor'=4] {'tensor'}, dimensions={2}, use_global_device_ids=true | all-gather | bytes 409600 | tf_op jit(solution)/shard_map/all_gather | solution.py:71
  33.9 3.0 %mul.125 = f32[64,6,2560]{2,1,0:T(8,128)} broadcast(f32[64,2560]{1,0:T(8,128)S(1)} %bitcast_convert_fusion), dimensions={0,2} | broadcast | bytes 4587520 | tf_op jit(solution)/shard_map/mul | solution.py:29
  36.9 5.1 %mul.126 = f32[384,2560]{1,0:T(8,128)} reshape(f32[64,6,2560]{2,1,0:T(8,128)} %mul.125) | data formatting | bytes 7864320 | tf_op jit(solution)/shard_map/mul | solution.py:29
  42.0 6.8 %scatter_custom_fusion = bf16[516,2560]{1,0:T(8,128)(2,1)} fusion(s32[384]{0:T(512)S(1)} %fusion.30, f32[384,2560]{1,0:T(8,128)} %mul.126, f32[384]{0:T(512)S(1)} %mul.123, bf16[]{:T(256)} %constant.32.clone.1), kind=kCustom, calls=%fused_computation.10 | custom fusion | flops 1966080 | bytes 6576130 | tf_op jit(solution)/shard_map/scatter | solution.py:31
  48.9 3.6 %reshape.216 = bf16[3,4,43,2560]{3,2,1,0:T(8,128)(2,1)} reshape(bf16[516,2560]{1,0:T(8,128)(2,1)} %scatter_custom_fusion) | data formatting | bytes 5283840 | tf_op jit(solution)/shard_map/reshape | solution.py:76
  52.5 3.6 %copy.52 = bf16[3,4,43,2560]{3,2,0,1:T(8,128)(2,1)} copy(bf16[3,4,43,2560]{3,2,1,0:T(8,128)(2,1)} %reshape.216) | data formatting | bytes 5283840 | tf_op jit(solution)/shard_map/reshape | solution.py:76
  56.1 6.5 %all-to-all-done = bf16[3,4,43,2560]{3,2,0,1:T(8,128)(2,1)S(1)} async-done(((bf16[3,4,43,2560]{3,2,0,1:T(8,128)(2,1)}), bf16[3,4,43,2560]{3,2,0,1:T(8,128)(2,1)S(1)}, u32[]{:S(2)}, u32[]{:S(2)}) %all-to-all-start) | async-done | bytes 2641952 | tf_op jit(solution)/shard_map/all_to_all | solution.py:65
  62.6 4.7 %all-to-all-start.1 = ((bf16[3,4,43,2560]{3,2,0,1:T(8,128)(2,1)}), bf16[3,4,43,2560]{3,2,0,1:T(8,128)(2,1)}, u32[]{:S(2)}, u32[]{:S(2)}) async-start(bf16[3,4,43,2560]{3,2,0,1:T(8,128)(2,1)} %copy.52), calls=%async_computation.2 | async-start | bytes 5898240 | tf_op jit(solution)/shard_map/all_to_all | solution.py:75
  67.3 0.2 reduce-scatter.2.cloned.1.call-start
  67.6 0.1 copy.40
  67.7 0.1 copy.41
  67.8 0.1 reduce_window_sum.17
  67.9 0.1 copy.43
  68.0 0.1 copy.44
  68.1 0.1 reduce_sum.51
  68.2 0.1 copy.56
  68.3 0.1 squeeze.25
  68.5 1.8 %copy.39 = bf16[3,4,43,2560]{3,2,1,0:T(8,128)(2,1)} copy(bf16[3,4,43,2560]{3,2,0,1:T(8,128)(2,1)S(1)} %all-to-all-done) | data formatting | bytes 5283840 | tf_op jit(solution)/shard_map/all_to_all | solution.py:65
  70.4 2.4 %reshape.215 = bf16[516,2560]{1,0:T(8,128)(2,1)S(1)} reshape(bf16[3,4,43,2560]{3,2,1,0:T(8,128)(2,1)} %copy.39) | data formatting | bytes 5283840 | tf_op jit(solution)/shard_map/reshape | solution.py:66
  72.8 3.3 %gather_fusion = bf16[384,2560]{1,0:T(8,128)(2,1)} fusion(bf16[516,2560]{1,0:T(8,128)(2,1)S(1)} %reshape.215, s32[1024]{0:T(1024)S(1)} %pad_clamp_fusion), kind=kCustom, calls=%fused_computation | custom fusion | bytes 3933696 | tf_op jit(solution)/shard_map/gather | solution.py:66
  76.1 4.5 %reshape.217 = f32[64,6,2560]{2,1,0:T(8,128)} reshape(bf16[384,2560]{1,0:T(8,128)(2,1)} %gather_fusion) | data formatting | bytes 5898240 | tf_op jit(solution)/shard_map/convert_element_type | solution.py:67
  80.5 4.4 %multiply_reduce_fusion = f32[64,2560]{1,0:T(8,128)S(1)} fusion(f32[64,6,2560]{2,1,0:T(8,128)} %reshape.217, f32[64,6]{1,0:T(8,128)S(1)} %bitcast.43), kind=kLoop, calls=%fused_computation.2 | loop fusion | flops 1802240 | bytes 4589056 | tf_op jit(solution)/shard_map/reduce_sum | solution.py:67
  85.0 0.0 all-gather.4.cloned.1.call-done
  85.0 2.9 %convolution_add_fusion = f32[64,2560]{1,0:T(8,128)} fusion(f32[64,2560]{1,0:T(8,128)S(1)} %multiply_reduce_fusion, bf16[1,384,2560]{2,1,0:T(8,128)(2,1)} %all-gather.4.cloned.1.call-done, bf16[1,64,384]{2,1,0:T(8,128)(2,1)S(1)} %copy-done), kind=kOutput, calls=%fused_computation.8 | convolution fusion | flops 125992960 | bytes 3325952 | tf_op jit(solution)/shard_map/dot_general | solution.py:55
  87.8 0.0 reduce-scatter.2.cloned.1.call-update
  87.9 14.3 %all-to-all-done.1 = bf16[3,4,43,2560]{3,2,0,1:T(8,128)(2,1)} async-done(((bf16[3,4,43,2560]{3,2,0,1:T(8,128)(2,1)}), bf16[3,4,43,2560]{3,2,0,1:T(8,128)(2,1)}, u32[]{:S(2)}, u32[]{:S(2)}) %all-to-all-start.1) | async-done | bytes 2641952 | tf_op jit(solution)/shard_map/all_to_all | solution.py:75
  102.2 4.5 %fusion.15 = bf16[1,3,4,43,256]{4,3,2,1,0:T(8,128)(2,1)S(1)} fusion(bf16[1,3,256,2560]{3,2,1,0:T(8,128)(2,1)} %param.12, bf16[3,4,43,2560]{3,2,0,1:T(8,128)(2,1)} %all-to-all-done.1), kind=kOutput, calls=%fused_computation.17 | convolution fusion | flops 676463616 | bytes 6838272 | tf_op jit(solution)/shard_map/egmd,ehd->egmh/dot_general | solution.py:82
  106.7 0.8 copy.54
  107.5 5.4 %reduce-scatter.2.cloned.1.call-done = f32[64,640]{1,0:T(8,128)} async-done(((f32[64,2560]{1,0:T(8,128)}), f32[64,640]{1,0:T(8,128)}) %reduce-scatter.2.cloned.1.call-update) | async-done | bytes 163856 | tf_op jit(solution)/shard_map/reduce_scatter | solution.py:68
  112.9 0.9 convert_element_type.36
  113.9 1.5 %collective-permute-start = (bf16[64,640]{1,0:T(8,128)(2,1)S(1)}, bf16[64,640]{1,0:T(8,128)(2,1)S(1)}, u32[]{:S(2)}, u32[]{:S(2)}) collective-permute-start(bf16[64,640]{1,0:T(8,128)(2,1)S(1)} %convert_element_type.36), channel_id=1, source_target_pairs={{0,16},{16,0},{1,17},{17,1},{2,18},{18,2},{3,19},{19,3},{4,20},{20... | collective-permute-start | bytes 245768 | tf_op jit(solution)/shard_map/ppermute | solution.py:10
  115.3 1.4 %fusion.23 = bf16[1,64,384]{2,1,0:T(8,128)(2,1)} fusion(bf16[1,384,2560]{2,1,0:T(8,128)(2,1)S(1)} %copy-done.1, bf16[1,64,2560]{2,1,0:T(8,128)(2,1)S(1)} %all-gather.1), kind=kOutput, calls=%fused_computation.19 | convolution fusion | flops 125853696 | bytes 2342912 | tf_op jit(solution)/shard_map/dot_general | solution.py:85
  116.7 1.7 %collective-permute-done = bf16[64,640]{1,0:T(8,128)(2,1)S(1)} collective-permute-done((bf16[64,640]{1,0:T(8,128)(2,1)S(1)}, bf16[64,640]{1,0:T(8,128)(2,1)S(1)}, u32[]{:S(2)}, u32[]{:S(2)}) %collective-permute-start) | collective-permute-done | bytes 81952 | tf_op jit(solution)/shard_map/ppermute | solution.py:10
  118.4 0.6 copy.72
  (26 shorter events, 0.3 us)
Async XLA Ops:
  7.2 77.8 %copy-start = (bf16[1,64,384]{2,1,0:T(8,128)(2,1)S(1)}, bf16[1,64,384]{2,1,0:T(8,128)(2,1)}, u32[]{:S(2)}) copy-start(bf16[1,64,384]{2,1,0:T(8,128)(2,1)} %param.13) | copy-start | bytes 147460
  7.2 77.8 %all-gather.4.cloned.1.call-start = ((), (), s32[]{:S(2)}) async-start(), calls=%async_computation.4 | async-start | bytes 2457600 | tf_op jit(solution)/shard_map/all_gather | solution.py:57
  12.8 4.4 %copy-start.3 = (s32[1,64,6]{1,0,2:T(1,128)S(1)}, s32[1,64,6]{1,0,2:T(1,128)}, u32[]{:S(2)}) copy-start(s32[1,64,6]{1,0,2:T(1,128)} %param.15) | copy-start | bytes 4612
  12.8 5.1 %copy-start.5 = (f32[1,64,6]{1,0,2:T(1,128)S(1)}, f32[1,64,6]{1,0,2:T(1,128)}, u32[]{:S(2)}) copy-start(f32[1,64,6]{1,0,2:T(1,128)} %param.16) | copy-start | bytes 4612
  12.8 5.5 %copy-start.2 = (bf16[1,64,640]{2,1,0:T(8,128)(2,1)S(1)}, bf16[1,64,640]{2,1,0:T(8,128)(2,1)}, u32[]{:S(2)}) copy-start(bf16[1,64,640]{2,1,0:T(8,128)(2,1)} %param.17) | copy-start | bytes 245764
  12.8 49.8 %all-to-all-start = ((bf16[3,4,43,2560]{3,2,0,1:T(8,128)(2,1)}), bf16[3,4,43,2560]{3,2,0,1:T(8,128)(2,1)S(1)}, u32[]{:S(2)}, u32[]{:S(2)}) async-start(bf16[3,4,43,2560]{3,2,0,1:T(8,128)(2,1)} %copy.38), calls=%async_computation | async-start | bytes 5898240 | tf_op jit(solution)/shard_map/all_to_all | solution.py:65
  56.1 11.5 %copy-start.4 = (s32[1,64,6]{1,0,2:T(1,128)S(1)}, s32[1,64,6]{1,0,2:T(1,128)}, u32[]{:S(2)}) copy-start(s32[1,64,6]{1,0,2:T(1,128)} %param.9) | copy-start | bytes 4612
  56.1 12.1 %copy-start.6 = (f32[1,64,6]{1,0,2:T(1,128)S(1)}, f32[1,64,6]{1,0,2:T(1,128)}, u32[]{:S(2)}) copy-start(f32[1,64,6]{1,0,2:T(1,128)} %param.10) | copy-start | bytes 4612
  62.6 39.5 %all-to-all-start.1 = ((bf16[3,4,43,2560]{3,2,0,1:T(8,128)(2,1)}), bf16[3,4,43,2560]{3,2,0,1:T(8,128)(2,1)}, u32[]{:S(2)}, u32[]{:S(2)}) async-start(bf16[3,4,43,2560]{3,2,0,1:T(8,128)(2,1)} %copy.52), calls=%async_computation.2 | async-start | bytes 5898240 | tf_op jit(solution)/shard_map/all_to_all | solution.py:75
  67.3 45.6 %reduce-scatter.2.cloned.1.call-start = ((), (), s32[]{:S(2)}) async-start(), calls=%async_computation.3 | async-start | bytes 819200 | tf_op jit(solution)/shard_map/reduce_scatter | solution.py:68
  87.9 27.5 %copy-start.1 = (bf16[1,384,2560]{2,1,0:T(8,128)(2,1)S(1)}, bf16[1,384,2560]{2,1,0:T(8,128)(2,1)}, u32[]{:S(2)}) copy-start(bf16[1,384,2560]{2,1,0:T(8,128)(2,1)} %all-gather.4.cloned.1.call-done) | copy-start | bytes 5898244
  113.9 4.5 %collective-permute-start = (bf16[64,640]{1,0:T(8,128)(2,1)S(1)}, bf16[64,640]{1,0:T(8,128)(2,1)S(1)}, u32[]{:S(2)}, u32[]{:S(2)}) collective-permute-start(bf16[64,640]{1,0:T(8,128)(2,1)S(1)} %convert_element_type.36), channel_id=1, source_target_pairs={{0,16},{16,0},{1,17},{17,1},{2,18},{18,2},{3,19},{19,3},{4,20},{20... | collective-permute-start | bytes 245768 | tf_op jit(solution)/shard_map/ppermute | solution.py:10
Sparse Core Ops, SparseCore 0:
  9.6 35.1 all-gather.3
  88.0 24.8 reduce-scatter.1
where the time goes:
time: 127 us; the launch traced here: 126 us
  local copies, waits for them, and re-layouts  32.2 us (25%)
  waiting for transfers between devices  28.6 us (23%)
  blocking collectives  15.6 us (12%)
  between operations  14.2 us (11%)
  other arithmetic  12.6 us (10%)
  matrix products  11.8 us (9%)
  starting transfers between devices  10.8 us (9%)
    all_gather x1, blocking collectives, on_device(): cotangent_whole = lax.all_gather(cotangent[0], 'tensor', axis=1, tiled=True)  15.6 us
    all_to_all x1, waiting for transfers between devices, on_device(): lax.all_to_all(outgoing.reshape(experts_here, groups, capacity, features)...  14.3 us
    mul x3, local copies, waits for them, and re-layouts, place_rows(): gates[:, :, None] * values[:, None, :].astype(jnp.float32)  8.23 us
    reshape x2, local copies, waits for them, and re-layouts, on_device(): outgoing.reshape(experts_here, groups, capacity, features)  7.22 us
    scatter x1, other arithmetic, place_rows(): return outgoing.at[positions].set(scaled.reshape(-1, values.shape[1]))  6.83 us
    all_to_all x1, waiting for transfers between devices, on_device(): lax.all_to_all(partial_value, 'expert', split_axis=1, concat_axis=1, tile...  6.55 us
    reduce_scatter x1, waiting for transfers between devices, on_device(): lax.psum_scatter(summand, 'tensor', scatter_dimension=1, tiled=True)  5.42 us
    all_to_all x1, starting transfers between devices, on_device(): lax.all_to_all(outgoing.reshape(experts_here, groups, capacity, features)...  4.66 us
  transfers between devices with their start and end apart: 5, of which 4 were waited for; matrix products, arithmetic and copies ran while one was open for 44% of the time, Pallas kernels for 0%

commit v1 on v0

--- a/solution.py
+++ b/solution.py
@@ -1,7 +1,281 @@
+import functools
+
 import jax
 import jax.numpy as jnp
 from jax import lax
+from jax.experimental import pallas as pl
+from jax.experimental.pallas import tpu as pltpu
 from jax.sharding import PartitionSpec as P
+
+MESH = pl.DeviceIdType.MESH
+LANES = 128
+F32 = jnp.float32
+BF16 = jnp.bfloat16
+
+
+def fused_kernel(
+    sizes,
+    fr_ref, fg_ref, br_ref, bg_ref,
+    hid_hbm, w_hbm, sh_hbm, sw_hbm, cot_hbm,
+    next_ref, hgrad_ref, sgrad_ref,
+    hid, w, sw, sh, cot, pack, hc, acc, keep,
+    s1_out, s1_in, s2_out, s2_in, s3_out, s3_in, s4_out,
+    back, sg_part, sg_out, sg_in,
+    send_sem, recv_sem, load_sem,
+):
+    (phases, ne, nt) = sizes
+    ph, e, z = lax.axis_index("phase"), lax.axis_index("expert"), lax.axis_index("tensor")
+    tok, top = fr_ref.shape
+    here, cap, hq = hid.shape[0] // ne, hid.shape[1], hid.shape[2]
+    dt = cot.shape[3]
+    hs = sw.shape[0]
+    experts = here * ne
+    core = lax.rem(e, 2)
+    sib = e + 1 - 2 * core
+    far = lax.rem(e + 2, ne)
+    far_sib = lax.rem(sib + 2, ne)
+    others_e = [lax.rem(e + r, ne) for r in range(1, ne)]
+    others_t = [lax.rem(z + d, nt) for d in range(1, nt)]
+
+    loads = [
+        pltpu.make_async_copy(hid_hbm, hid, load_sem.at[0]),
+        pltpu.make_async_copy(w_hbm, w, load_sem.at[1]),
+        pltpu.make_async_copy(sw_hbm, sw, load_sem.at[2]),
+        pltpu.make_async_copy(sh_hbm, sh.at[e], load_sem.at[3]),
+        pltpu.make_async_copy(cot_hbm, cot.at[z, e], load_sem.at[4]),
+    ]
+    for i in (4, 3, 0, 1, 2):
+        loads[i].start()
+
+    barrier = pltpu.get_barrier_semaphore()
+    partners = [{"expert": o} for o in others_e] + [{"tensor": o} for o in others_t]
+    ahead, behind = lax.rem(ph + 1, phases), lax.rem(ph + phases - 1, phases)
+    partners.append({"phase": ahead})
+    if phases > 2:
+        partners.append({"phase": behind})
+    for partner in partners:
+        pl.semaphore_signal(barrier, inc=1, device_id=partner, device_id_type=MESH)
+
+    lane = lax.broadcasted_iota(jnp.int32, (tok, LANES), 1)
+    hot = jnp.zeros((tok, LANES), F32)
+    gate = jnp.zeros((tok, LANES), F32)
+    for direction, (routes, gates) in enumerate(((fr_ref, fg_ref), (br_ref, bg_ref))):
+        base = 2 * direction * experts
+        for k in range(top):
+            named = routes[:, k:k + 1] + base
+            hot = jnp.where(named == lane, 1.0, hot)
+            gate = jnp.where(named + experts == lane, gates[:, k:k + 1], gate)
+    row = lax.broadcasted_iota(jnp.int32, (tok, tok), 0)
+    column = lax.broadcasted_iota(jnp.int32, (tok, tok), 1)
+    earlier = jnp.where(row > column, 1.0, 0.0).astype(BF16)
+    slots = jnp.dot(earlier, hot.astype(BF16), preferred_element_type=F32)
+    is_slot = (lane < experts) | ((lane >= 2 * experts) & (lane < 3 * experts))
+    pack[e] = jnp.where(is_slot, jnp.where(hot > 0.5, slots, -1.0), gate)
+
+    copies = []
+
+    def send(src, dst, to):
+        i = len(copies)
+        copy = pltpu.make_async_remote_copy(
+            src_ref=src, dst_ref=dst, send_sem=send_sem.at[i], recv_sem=recv_sem.at[i],
+            device_id=to, device_id_type=MESH,
+        )
+        copy.start()
+        copies.append(copy)
+        return copy
+
+    pl.semaphore_wait(barrier, len(partners))
+    pack_copies = [send(pack.at[e], pack.at[e], {"expert": o}) for o in others_e]
+    loads[4].wait()
+    mine = cot.at[z, e]
+    z_copies = [send(mine, mine, {"tensor": o}) for o in others_t]
+    y_copies = [send(mine, mine, {"expert": far})]
+    sib_copies = [send(mine, mine, {"expert": sib})]
+    loads[3].wait()
+    sh_copies = [send(sh.at[e], sh.at[e], {"expert": o}) for o in others_e]
+
+    order = (far_sib, sib, far, e)
+    slot_at = lax.broadcasted_iota(jnp.int32, (tok, cap), 1).astype(F32)
+
+    def pick(table, at):
+        return jnp.sum(jnp.where(lane == at, table, 0.0), axis=1, keepdims=True)
+
+    for copy in pack_copies:
+        copy.wait_recv()
+    loads[0].wait()
+    for n, b in enumerate(order):
+        table = pack[b]
+        for i in range(here):
+            x = e * here + i
+            place = jnp.where(pick(table, x) == slot_at, 1.0, 0.0).astype(BF16)
+            rows = jnp.dot(place, hid[i * ne + b], preferred_element_type=F32)
+            hc[n * tok:(n + 1) * tok, i * hq:(i + 1) * hq] = (
+                rows * pick(table, experts + x)
+            ).astype(BF16)
+
+    def relay(d):
+        z_copies[d - 1].wait_recv()
+        piece = cot.at[lax.rem(z + nt - d, nt), e]
+        y_copies.append(send(piece, piece, {"expert": far}))
+        sib_copies.append(send(piece, piece, {"expert": sib}))
+
+    loads[1].wait()
+    loads[2].wait()
+    for copy in sh_copies:
+        copy.wait_recv()
+    s1, s2, s3 = [], [], []
+    for s in range(nt):
+        f = lax.rem(z + 1 + s, nt)
+        cols = pl.ds(pl.multiple_of(f * dt, LANES), dt)
+        acc[...] = jnp.dot(hc[...], w[:, cols], preferred_element_type=F32)
+
+        @pl.when(f == e)
+        def _():
+            shared = jnp.concatenate([sh[b] for b in order], axis=0)
+            acc[...] += jnp.dot(shared, sw[...], preferred_element_type=F32)
+
+        for g in range(2):
+            s1_out[s, g] = acc[g * tok:(g + 1) * tok, :].astype(BF16)
+        s1.append(send(s1_out.at[s], s1_in.at[s], {"expert": sib}))
+        for g in range(2):
+            keep[s, g] = acc[(2 + g) * tok:(3 + g) * tok, :]
+        if s >= 1:
+            relay(s)
+    for s in range(nt):
+        s1[s].wait_recv()
+        s2_out[s] = (keep[s, 0] + s1_in[s, 0].astype(F32)).astype(BF16)
+        s2.append(send(s2_out.at[s], s2_in.at[s], {"expert": far}))
+        keep[s, 1] = keep[s, 1] + s1_in[s, 1].astype(F32)
+
+    far_copies = []
+
+    def hand_over(d):
+        y_copies[d].wait_recv()
+        piece = cot.at[lax.rem(z + nt - d, nt), far]
+        far_copies.append(send(piece, piece, {"expert": sib}))
+
+    def back_part(d):
+        f = lax.rem(z + nt - d, nt)
+        sib_copies[d].wait_recv()
+        far_copies[d].wait_recv()
+        cols = pl.ds(pl.multiple_of(f * dt, LANES), dt)
+        rows = cot[f].reshape(ne * tok, dt)
+        part = lax.dot_general(
+            rows, w[:, cols], (((1,), (1,)), ((), ())), preferred_element_type=F32
+        )
+        if d == 0:
+            back[...] = part
+        else:
+            back[...] += part
+
+    def reduce_z(s):
+        s2[s].wait_recv()
+        total = keep[s, 1] + s2_in[s].astype(F32)
+        if s < nt - 1:
+            s3_out[s] = total.astype(BF16)
+            s3.append(send(s3_out.at[s], s3_in.at[s], {"tensor": others_t[s]}))
+        else:
+            keep[s, 1] = total
+
+    for d in range(nt):
+        hand_over(d)
+        reduce_z(d)
+    for d in range(nt):
+        back_part(d)
+
+    sg_part[...] = lax.dot_general(
+        cot[e].reshape(ne * tok, dt), sw[...], (((1,), (1,)), ((), ())),
+        preferred_element_type=F32,
+    ).reshape(ne, tok, hs)
+    sg = []
+    for r, o in enumerate(others_e):
+        sg_out[r] = sg_part[o].astype(BF16)
+        sg.append(send(sg_out.at[r], sg_in.at[r], {"expert": o}))
+
+    total = keep[nt - 1, 1]
+    for s in range(nt - 1):
+        s3[s].wait_recv()
+        total = total + s3_in[s].astype(F32)
+    s4_out[...] = total.astype(BF16)
+    s4 = send(s4_out, next_ref, {"phase": ahead})
+
+    for b in range(ne):
+        table = pack[b]
+        for i in range(here):
+            x = 2 * experts + e * here + i
+            place = jnp.where(pick(table, x) == slot_at, 1.0, 0.0).astype(BF16)
+            rows = back[b * tok:(b + 1) * tok, i * hq:(i + 1) * hq]
+            rows = (rows * pick(table, experts + x)).astype(BF16)
+            hgrad_ref[i * ne + b] = lax.dot_general(
+                place, rows, (((0,), (0,)), ((), ())), preferred_element_type=F32
+            ).astype(BF16)
+
+    shared_total = sg_part[e]
+    for copy in sg:
+        copy.wait_recv()
+    for r in range(ne - 1):
+        shared_total = shared_total + sg_in[r].astype(F32)
+    sgrad_ref[...] = shared_total.astype(BF16)
+    s4.wait_recv()
+    for copy in copies:
+        copy.wait_send()
+
+
+def fused(sizes, fr, fg, hidden, weight, shared, sweight, br, bg, cot):
+    phases, ne, nt = sizes
+    here, groups, cap, hq = hidden.shape[1:]
+    tok = fr.shape[1]
+    features = weight.shape[3]
+    dt = cot.shape[2]
+    hs = shared.shape[2]
+    vmem = pl.BlockSpec(memory_space=pltpu.VMEM)
+    anywhere = pl.BlockSpec(memory_space=pl.ANY)
+    copies = 3 * (ne - 1) + 2 * (nt - 1) + 6 * nt - nt + 1
+    rows = ne * tok
+    handed, hgrad, sgrad = pl.pallas_call(
+        functools.partial(fused_kernel, sizes),
+        out_shape=(
+            jax.ShapeDtypeStruct((tok, dt), BF16),
+            jax.ShapeDtypeStruct((here * groups, cap, hq), BF16),
+            jax.ShapeDtypeStruct((tok, hs), BF16),
+        ),
+        in_specs=[vmem] * 4 + [anywhere] * 5,
+        out_specs=(vmem, vmem, vmem),
+        scratch_shapes=[
+            pltpu.VMEM((here * groups, cap, hq), BF16),
+            pltpu.VMEM((here * hq, features), BF16),
+            pltpu.VMEM((hs, dt), BF16),
+            pltpu.VMEM((ne, tok, hs), BF16),
+            pltpu.VMEM((nt, ne, tok, dt), BF16),
+            pltpu.VMEM((ne, tok, LANES), F32),
+            pltpu.VMEM((rows, here * hq), BF16),
+            pltpu.VMEM((rows, dt), F32),
+            pltpu.VMEM((nt, 2, tok, dt), F32),
+            pltpu.VMEM((nt, 2, tok, dt), BF16),
+            pltpu.VMEM((nt, 2, tok, dt), BF16),
+            pltpu.VMEM((nt, tok, dt), BF16),
+            pltpu.VMEM((nt, tok, dt), BF16),
+            pltpu.VMEM((nt - 1, tok, dt), BF16),
+            pltpu.VMEM((nt - 1, tok, dt), BF16),
+            pltpu.VMEM((tok, dt), BF16),
+            pltpu.VMEM((rows, here * hq), F32),
+            pltpu.VMEM((ne, tok, hs), F32),
+            pltpu.VMEM((ne - 1, tok, hs), BF16),
+            pltpu.VMEM((ne - 1, tok, hs), BF16),
+            pltpu.SemaphoreType.DMA((copies,)),
+            pltpu.SemaphoreType.DMA((copies,)),
+            pltpu.SemaphoreType.DMA((5,)),
+        ],
+        compiler_params=pltpu.CompilerParams(
+            collective_id=0, has_side_effects=True, vmem_limit_bytes=48 * 1024 * 1024
+        ),
+    )(
+        fr[0], fg[0], br[0], bg[0],
+        hidden.reshape(here * groups, cap, hq),
+        weight.reshape(here * hq, features),
+        shared[0], sweight[0], cot[0],
+    )
+    return handed[None], hgrad.reshape(hidden.shape), sgrad[None]
 
 
 def shifted(value, axis, steps):
@@ -31,7 +305,7 @@
     return outgoing.at[positions].set(scaled.reshape(-1, values.shape[1]))
 
 
-def on_device(
+def unfused(
     forward_routes,
     forward_gates,
     hidden_rows,
@@ -92,6 +366,17 @@
 
 
 def solution(mesh):
+    sizes = tuple(mesh.shape[axis] for axis in ("phase", "expert", "tensor"))
+
+    def on_device(*arrays):
+        phases, ne, nt = sizes
+        hidden, weight, cot = arrays[2], arrays[3], arrays[8]
+        two_chips = ne == 4 and ne == nt and phases > 1
+        fits = 4 * ne * weight.shape[1] <= LANES and cot.shape[2] % LANES == 0
+        if two_chips and fits:
+            return fused(sizes, *arrays)
+        return unfused(*arrays)
+
     return jax.shard_map(
         on_device,
         mesh=mesh,

time: 127 us -> 48 us (0.38)
  Pallas kernels: 0 us -> 35.9 us
  waiting for transfers between devices: 28.6 us -> 0 us
  local copies, waits for them, and re-layouts: 32.2 us -> 11 us
  blocking collectives: 15.6 us -> 0 us
  between operations: 14.2 us -> 0.66 us
  other arithmetic: 12.6 us -> 0 us
  matrix products: 11.8 us -> 0 us
  starting transfers between devices: 10.8 us -> 0 us
    pallas_call x0 -> x1, Pallas kernels: none -> 35.9 us  [fused(): pl.pallas_call(functools.partial(fused_kernel, sizes), out_shape=(jax.Sha...]
    all_to_all x2 -> x0, waiting for transfers between devices: 20.8 us -> none  [the longest x1 14.3 us: on_device(): lax.all_to_all(outgoing.reshape(experts_here, groups, capacity, features)...]
    all_gather x1 -> x0, blocking collectives: 15.6 us -> none  [on_device(): cotangent_whole = lax.all_gather(cotangent[0], 'tensor', axis=1, tiled=True)]
    dot_general x4 -> x0, matrix products: 11.8 us -> none  [the longest x1 4.48 us: on_device(): jnp.einsum('egmd,ehd->egmh', received, weight, preferred_element_type=jnp...]
    reshape x3 -> x0, local copies, waits for them, and re-layouts: 9.63 us -> none  [the longest x2 7.22 us: on_device(): outgoing.reshape(experts_here, groups, capacity, features)]
    unnamed x21 -> x16, local copies, waits for them, and re-layouts: 1.8 us -> 11 us
    all_to_all x2 -> x0, starting transfers between devices: 9.06 us -> none  [the longest x1 4.66 us: on_device(): lax.all_to_all(outgoing.reshape(experts_here, groups, capacity, features)...]
    mul x4 -> x0, local copies, waits for them, and re-layouts: 8.33 us -> none  [the longest x3 8.23 us: place_rows(): gates[:, :, None] * values[:, None, :].astype(jnp.float32)]
  transfers between devices with their start and end apart: 5 -> 0, of which waited for: 4 -> 0; matrix products, arithmetic and copies ran while one was open for 44% -> 0% of each run, Pallas kernels for 0% -> 0%
where the time goes in v1:
time: 48 us; the launch traced here: 47.5 us
  Pallas kernels  35.9 us (75%)
  local copies, waits for them, and re-layouts  11 us (23%)
  between operations  0.66 us (1%)
    pallas_call x1, Pallas kernels, fused(): pl.pallas_call(functools.partial(fused_kernel, sizes), out_shape=(jax.Sha...  35.9 us
    unnamed x16, local copies, waits for them, and re-layouts  11 us

profile of v1, /device:TPU:0, one launch (start us, length us, event | category | flops | bytes accessed | tf_op | source)
XLA Modules:
  0.0 47.5 jit_solution(1419728512230672518)
XLA Ops:
  0.6 0.8 %copy.12 = s32[1,64,6]{2,1,0:T(8,128)S(1)} copy(s32[1,64,6]{1,0,2:T(1,128)} %param.9) | data formatting | bytes 3072 | tf_op args[0]
  1.4 0.8 %copy.13 = f32[1,64,6]{2,1,0:T(8,128)S(1)} copy(f32[1,64,6]{1,0,2:T(1,128)} %param.10) | data formatting | bytes 3072 | tf_op args[1]
  2.2 0.8 %copy.14 = s32[1,64,6]{2,1,0:T(8,128)S(1)} copy(s32[1,64,6]{1,0,2:T(1,128)} %param.15) | data formatting | bytes 3072 | tf_op args[6]
  3.0 0.8 %copy.15 = f32[1,64,6]{2,1,0:T(8,128)S(1)} copy(f32[1,64,6]{1,0,2:T(1,128)} %param.16) | data formatting | bytes 3072 | tf_op args[7]
  3.7 1.0 %copy.16 = bf16[1,3,4,43,256]{4,3,2,1,0:T(8,128)(2,1)S(1)} copy(bf16[1,3,4,43,256]{4,2,3,1,0:T(4,128)(2,1)} %param.11) | data formatting | bytes 528384 | tf_op args[2]
  4.7 0.0 copy-start
  4.7 2.1 %copy-done = bf16[1,3,256,2560]{3,2,1,0:T(8,128)(2,1)S(1)} copy-done((bf16[1,3,256,2560]{3,2,1,0:T(8,128)(2,1)S(1)}, bf16[1,3,256,2560]{3,2,1,0:T(8,128)(2,1)}, u32[]{:S(2)}) %copy-start) | copy-done | bytes 3932184
  6.8 0.0 copy-start.1
  6.8 1.0 %copy-done.1 = bf16[1,384,640]{2,1,0:T(8,128)(2,1)S(1)} copy-done((bf16[1,384,640]{2,1,0:T(8,128)(2,1)S(1)}, bf16[1,384,640]{2,1,0:T(8,128)(2,1)}, u32[]{:S(2)}) %copy-start.1) | copy-done | bytes 491544
  7.9 0.0 copy-start.2
  7.9 0.9 %copy-done.2 = bf16[1,64,640]{2,1,0:T(8,128)(2,1)S(1)} copy-done((bf16[1,64,640]{2,1,0:T(8,128)(2,1)S(1)}, bf16[1,64,640]{2,1,0:T(8,128)(2,1)}, u32[]{:S(2)}) %copy-start.2) | copy-done | bytes 81944
  8.7 0.0 copy-start.3
  8.7 0.8 %copy-done.3 = bf16[1,64,384]{2,1,0:T(8,128)(2,1)S(1)} copy-done((bf16[1,64,384]{2,1,0:T(8,128)(2,1)S(1)}, bf16[1,64,384]{2,1,0:T(8,128)(2,1)}, u32[]{:S(2)}) %copy-start.3) | copy-done | bytes 49176
  9.5 35.9 %shard_map.112 = (bf16[64,640]{1,0:T(8,128)(2,1)S(1)}, bf16[12,43,256]{2,1,0:T(8,128)(2,1)S(1)}, bf16[64,384]{1,0:T(8,128)(2,1)S(1)}) custom-call(s32[64,6]{1,0:T(8,128)S(1)} %bitcast.16, f32[64,6]{1,0:T(8,128)S(1)} %bitcast.17, s32[64,6]{1,0:T(8,128)S(1)} %bitcast.18, f32[64,6]{1,0:T(8,128)S(1)} %bitcast.19, bf16[12,43,256]{2,1,0:T(8,128)(2,1)S(1)} %bitcast.13, ...), custom_call_target="tpu_custom_call" | custom-call | tf_op jit(solution)/shard_map/pallas_call | solution.py:235
  45.4 0.8 %copy.17 = bf16[1,3,4,43,256]{4,2,3,1,0:T(4,128)(2,1)} copy(bf16[1,3,4,43,256]{4,3,2,1,0:T(8,128)(2,1)S(1)} %bitcast.15) | data formatting | bytes 528384
  46.3 0.6 %copy.20 = bf16[1,64,640]{2,1,0:T(8,128)(2,1)} copy(bf16[1,64,640]{2,1,0:T(8,128)(2,1)S(1)} %bitcast.20) | data formatting | bytes 163840
  46.9 0.6 %copy.21 = bf16[1,64,384]{2,1,0:T(8,128)(2,1)} copy(bf16[1,64,384]{2,1,0:T(8,128)(2,1)S(1)} %bitcast.23) | data formatting | bytes 98304
Async XLA Ops:
  4.7 2.1 %copy-start = (bf16[1,3,256,2560]{3,2,1,0:T(8,128)(2,1)S(1)}, bf16[1,3,256,2560]{3,2,1,0:T(8,128)(2,1)}, u32[]{:S(2)}) copy-start(bf16[1,3,256,2560]{3,2,1,0:T(8,128)(2,1)} %param.12) | copy-start | bytes 11796484
  6.8 1.0 %copy-start.1 = (bf16[1,384,640]{2,1,0:T(8,128)(2,1)S(1)}, bf16[1,384,640]{2,1,0:T(8,128)(2,1)}, u32[]{:S(2)}) copy-start(bf16[1,384,640]{2,1,0:T(8,128)(2,1)} %param.14) | copy-start | bytes 1474564
  7.9 0.9 %copy-start.2 = (bf16[1,64,640]{2,1,0:T(8,128)(2,1)S(1)}, bf16[1,64,640]{2,1,0:T(8,128)(2,1)}, u32[]{:S(2)}) copy-start(bf16[1,64,640]{2,1,0:T(8,128)(2,1)} %param.17) | copy-start | bytes 245764
  8.7 0.8 %copy-start.3 = (bf16[1,64,384]{2,1,0:T(8,128)(2,1)S(1)}, bf16[1,64,384]{2,1,0:T(8,128)(2,1)}, u32[]{:S(2)}) copy-start(bf16[1,64,384]{2,1,0:T(8,128)(2,1)} %param.13) | copy-start | bytes 147460

commit v2 on v1

v2 whole, which is shorter than its diff:
```python
import functools

import jax
import jax.numpy as jnp
from jax import lax
from jax.experimental import pallas as pl
from jax.experimental.pallas import tpu as pltpu
from jax.sharding import PartitionSpec as P

MESH = pl.DeviceIdType.MESH
LANES = 128
F32 = jnp.float32
BF16 = jnp.bfloat16


def fused_kernel(
    sizes,
    fr_hbm, fg_hbm, br_hbm, bg_hbm,
    hid_hbm, w_hbm, sh_hbm, sw_hbm, cot_hbm,
    next_ref, hgrad_ref, sgrad_ref,
    fr, fg, br, bg,
    hid, w, sw, sh, cot, pack, hc, acc, keep,
    s1_out, s1_in, s2_out, s2_in, s3_out, s3_in,
    back, sg_part, sg_out, sg_in, sg_out2, sg_in2,
    send_sem, recv_sem, load_sem,
):
    phases, ne, nt = sizes
    ph, e, z = lax.axis_index("phase"), lax.axis_index("expert"), lax.axis_index("tensor")
    top, _, tok = fr.shape
    here, cap, _, hq = hid.shape
    dt = cot.shape[3]
    hs = sw.shape[0]
    experts = here * ne
    slots_all = cap * ne
    core = lax.rem(e, 2)
    sib = e + 1 - 2 * core
    far = lax.rem(e + 2, ne)
    far_sib = lax.rem(sib + 2, ne)
    others_t = [lax.rem(z + d, nt) for d in range(1, nt)]
    ahead, behind = lax.rem(ph + 1, phases), lax.rem(ph + phases - 1, phases)

    pairs = (
        (fr_hbm, fr), (fg_hbm, fg), (br_hbm, br), (bg_hbm, bg),
        (cot_hbm, cot.at[z, e]), (sh_hbm, sh.at[e]), (hid_hbm, hid), (w_hbm, w), (sw_hbm, sw),
    )
    loads = [pltpu.make_async_copy(a, b, load_sem.at[i]) for i, (a, b) in enumerate(pairs)]
    for load in loads:
        load.start()

    barrier = pltpu.get_barrier_semaphore()
    partners = [{"expert": sib}, {"expert": far}] + [{"tensor": o} for o in others_t]
    for step in range(nt):
        partners.append({"phase": ahead, "tensor": lax.rem(z + step, nt)})
        if phases > 2:
            partners.append({"phase": behind, "tensor": lax.rem(z + step, nt)})
    for partner in partners:
        pl.semaphore_signal(barrier, inc=1, device_id=partner, device_id_type=MESH)

    for load in loads[:4]:
        load.wait()
    across = 2 * experts
    level = lax.broadcasted_iota(jnp.int32, (across, 2 * tok), 0)
    hot = jnp.zeros((across, 2 * tok), F32)
    gate = jnp.zeros((across, 2 * tok), F32)
    for k in range(top):
        named = jnp.concatenate([fr[k], br[k]], axis=1)
        weigh = jnp.concatenate([fg[k], bg[k]], axis=1)
        hot = jnp.where(named == level, 1.0, hot)
        gate = jnp.where(named + experts == level, weigh, gate)
    first = lax.broadcasted_iota(jnp.int32, (2 * tok, 2 * tok), 0)
    second = lax.broadcasted_iota(jnp.int32, (2 * tok, 2 * tok), 1)
    earlier = (first < second) & ((first < tok) == (second < tok))
    counts = jnp.dot(
        hot.astype(BF16), jnp.where(earlier, 1.0, 0.0).astype(BF16), preferred_element_type=F32
    )
    pack[e] = jnp.where(level < experts, jnp.where(hot > 0.5, counts, -1.0), gate)

    copies = []

    def send(src, dst, to):
        i = len(copies)
        copy = pltpu.make_async_remote_copy(
            src_ref=src, dst_ref=dst, send_sem=send_sem.at[i], recv_sem=recv_sem.at[i],
            device_id=to, device_id_type=MESH,
        )
        copy.start()
        copies.append(copy)
        return copy

    def spread(buffer):
        return [send(buffer.at[e], buffer.at[e], {"expert": o}) for o in (far, sib)]

    def hand_on(buffer, pair):
        pair[0].wait_recv()
        pair.append(send(buffer.at[far], buffer.at[far], {"expert": sib}))

    pl.semaphore_wait(barrier, len(partners))
    pack_copies = spread(pack)
    loads[5].wait()
    sh_copies = spread(sh)
    loads[4].wait()
    mine = cot.at[z, e]
    z_copies = [send(mine, mine, {"tensor": o}) for o in others_t]
    y_copies = [send(mine, mine, {"expert": far})]
    sib_copies = [send(mine, mine, {"expert": sib})]
    hand_on(pack, pack_copies)
    hand_on(sh, sh_copies)

    order = (far_sib, sib, far, e)
    level = lax.broadcasted_iota(jnp.int32, (tok, across), 1)
    entry = lax.broadcasted_iota(jnp.int32, (tok, slots_all), 1).astype(F32)

    def pick(table, at):
        return jnp.sum(jnp.where(level == at, table, 0.0), axis=1, keepdims=True)

    pack_copies[1].wait_recv()
    pack_copies[2].wait_recv()
    loads[6].wait()
    hidden = [hid[i].reshape(slots_all, hq) for i in range(here)]
    for n, b in enumerate(order):
        table = pack[b].T[:tok]
        offset = b.astype(F32)
        for i in range(here):
            x = e * here + i
            place = jnp.where(pick(table, x) * ne + offset == entry, 1.0, 0.0).astype(BF16)
            rows = jnp.dot(place, hidden[i], preferred_element_type=F32)
            hc[n * tok:(n + 1) * tok, i * hq:(i + 1) * hq] = (
                rows * pick(table, experts + x)
            ).astype(BF16)

    def relay(d):
        z_copies[d - 1].wait_recv()
        piece = cot.at[lax.rem(z + nt - d, nt), e]
        y_copies.append(send(piece, piece, {"expert": far}))
        sib_copies.append(send(piece, piece, {"expert": sib}))

    relay(1)
    loads[7].wait()
    loads[8].wait()
    sh_copies[1].wait_recv()
    sh_copies[2].wait_recv()
    s1, s2, s3 = [], [], []
    for s in range(nt):
        f = lax.rem(z + 1 + s, nt)
        cols = pl.ds(pl.multiple_of(f * dt, LANES), dt)
        acc[...] = jnp.dot(hc[...], w[:, cols], preferred_element_type=F32)

        @pl.when(f == e)
        def _():
            shared = jnp.concatenate([sh[b] for b in order], axis=0)
            acc[...] += jnp.dot(shared, sw[...], preferred_element_type=F32)

        for g in range(2):
            s1_out[s, g] = acc[g * tok:(g + 1) * tok, :].astype(BF16)
        s1.append(send(s1_out.at[s], s1_in.at[s], {"expert": sib}))
        for g in range(2):
            keep[s, g] = acc[(2 + g) * tok:(3 + g) * tok, :]
        if 1 <= s < nt - 1:
            relay(s + 1)
    for s in range(nt):
        s1[s].wait_recv()
        s2_out[s] = (keep[s, 0] + s1_in[s, 0].astype(F32)).astype(BF16)
        s2.append(send(s2_out.at[s], s2_in.at[s], {"expert": far}))
        keep[s, 1] = keep[s, 1] + s1_in[s, 1].astype(F32)

    far_copies = []
    for d in range(nt):
        y_copies[d].wait_recv()
        piece = cot.at[lax.rem(z + nt - d, nt), far]
        far_copies.append(send(piece, piece, {"expert": sib}))

    for d in range(nt):
        f = lax.rem(z + nt - d, nt)
        sib_copies[d].wait_recv()
        far_copies[d].wait_recv()
        cols = pl.ds(pl.multiple_of(f * dt, LANES), dt)
        part = lax.dot_general(
            cot[f].reshape(ne * tok, dt), w[:, cols], (((1,), (1,)), ((), ())),
            preferred_element_type=F32,
        )
        if d == 0:
            back[...] = part
        else:
            back[...] += part

    sg_part[...] = lax.dot_general(
        cot[e].reshape(ne * tok, dt), sw[...], (((1,), (1,)), ((), ())),
        preferred_element_type=F32,
    ).reshape(ne, tok, hs)
    for g in range(2):
        sg_out[g] = sg_part[order[g]].astype(BF16)
    sg = send(sg_out, sg_in, {"expert": sib})

    def reduce_z(s):
        s2[s].wait_recv()
        s3_out[s] = (keep[s, 1] + s2_in[s].astype(F32)).astype(BF16)
        to = {"phase": ahead, "tensor": others_t[s] if s < nt - 1 else z}
        s3.append(send(s3_out.at[s], s3_in.at[s], to))

    def rows_back(i):
        x = e * here + i
        at = [pack[b, pl.ds(x, 1), :][:, tok:] for b in range(ne)]
        named = jnp.concatenate([a * ne + b for b, a in enumerate(at)], axis=1)
        entry_down = lax.broadcasted_iota(jnp.int32, (slots_all, ne * tok), 0).astype(F32)
        place = jnp.where(named == entry_down, 1.0, 0.0).astype(BF16)
        gates = jnp.concatenate([pick(pack[b].T[tok:], experts + x) for b in range(ne)], axis=0)
        rows = (back[:, i * hq:(i + 1) * hq] * gates).astype(BF16)
        hgrad_ref[i] = jnp.dot(place, rows, preferred_element_type=F32).astype(BF16).reshape(
            cap, ne, hq
        )

    reduce_z(0)
    rows_back(0)
    sg.wait_recv()
    sg_out2[...] = (sg_part[far] + sg_in[0].astype(F32)).astype(BF16)
    sg2 = send(sg_out2, sg_in2, {"expert": far})
    reduce_z(1)
    for i in range(1, here):
        rows_back(i)
    for s in range(2, nt):
        reduce_z(s)
    sg2.wait_recv()
    sgrad_ref[...] = (
        sg_part[e] + sg_in[1].astype(F32) + sg_in2[...].astype(F32)
    ).astype(BF16)
    total = jnp.zeros(next_ref.shape, F32)
    for s in range(nt):
        s3[s].wait_recv()
        total = total + s3_in[s].astype(F32)
    next_ref[...] = total.astype(BF16)
    for copy in copies:
        copy.wait_send()


def store_kernel(*refs):
    count = len(refs) // 2
    sems = refs[-1]
    moves = [
        pltpu.make_async_copy(refs[i], refs[count + i], sems.at[i]) for i in range(count)
    ]
    for move in moves:
        move.start()
    for move in moves:
        move.wait()


def fused(sizes, fr, fg, hidden, weight, shared, sweight, br, bg, cot):
    phases, ne, nt = sizes
    here, groups, cap, hq = hidden.shape[1:]
    tok, top = fr.shape[1:]
    features = weight.shape[3]
    dt = cot.shape[2]
    hs = shared.shape[2]
    vmem = pl.BlockSpec(memory_space=pltpu.VMEM)
    hbm = pl.BlockSpec(memory_space=pltpu.HBM)
    copies = 6 + (nt - 1) + 6 * nt + 2
    rows = ne * tok
    results = (
        jax.ShapeDtypeStruct((tok, dt), BF16),
        jax.ShapeDtypeStruct((here, cap, groups, hq), BF16),
        jax.ShapeDtypeStruct((tok, hs), BF16),
    )
    made = pl.pallas_call(
        functools.partial(fused_kernel, sizes),
        out_shape=results,
        in_specs=[hbm] * 9,
        out_specs=(vmem, vmem, vmem),
        scratch_shapes=[
            pltpu.VMEM((top, 1, tok), jnp.int32),
            pltpu.VMEM((top, 1, tok), F32),
            pltpu.VMEM((top, 1, tok), jnp.int32),
            pltpu.VMEM((top, 1, tok), F32),
            pltpu.VMEM((here, cap, groups, hq), BF16),
            pltpu.VMEM((here * hq, features), BF16),
            pltpu.VMEM((hs, dt), BF16),
            pltpu.VMEM((ne, tok, hs), BF16),
            pltpu.VMEM((nt, ne, tok, dt), BF16),
            pltpu.VMEM((ne, 2 * here * ne, 2 * tok), F32),
            pltpu.VMEM((rows, here * hq), BF16),
            pltpu.VMEM((rows, dt), F32),
            pltpu.VMEM((nt, 2, tok, dt), F32),
            pltpu.VMEM((nt, 2, tok, dt), BF16),
            pltpu.VMEM((nt, 2, tok, dt), BF16),
            pltpu.VMEM((nt, tok, dt), BF16),
            pltpu.VMEM((nt, tok, dt), BF16),
            pltpu.VMEM((nt, tok, dt), BF16),
            pltpu.VMEM((nt, tok, dt), BF16),
            pltpu.VMEM((rows, here * hq), F32),
            pltpu.VMEM((ne, tok, hs), F32),
            pltpu.VMEM((2, tok, hs), BF16),
            pltpu.VMEM((2, tok, hs), BF16),
            pltpu.VMEM((tok, hs), BF16),
            pltpu.VMEM((tok, hs), BF16),
            pltpu.SemaphoreType.DMA((copies,)),
            pltpu.SemaphoreType.DMA((copies,)),
            pltpu.SemaphoreType.DMA((9,)),
        ],
        compiler_params=pltpu.CompilerParams(
            collective_id=0, has_side_effects=True, vmem_limit_bytes=32 * 1024 * 1024
        ),
    )(
        *(a.transpose(2, 0, 1) for a in (fr, fg, br, bg)),
        hidden[0].transpose(0, 2, 1, 3),
        weight.reshape(here * hq, features),
        shared[0], sweight[0], cot[0],
    )
    handed, hgrad, sgrad = pl.pallas_call(
        store_kernel,
        out_shape=results,
        in_specs=[vmem] * 3,
        out_specs=[hbm] * 3,
        scratch_shapes=[pltpu.SemaphoreType.DMA((3,))],
    )(*made)
    return handed[None], hgrad.transpose(0, 2, 1, 3)[None], sgrad[None]


def shifted(value, axis, steps):
    count = lax.axis_size(axis)
    pairs = [(source, (source + steps) % count) for source in range(count)]
    return lax.ppermute(value, axis, pairs)


def slot_numbers(routes, experts):
    numbers = jnp.arange(experts, dtype=jnp.int32)
    onehot = (routes[:, :, None] == numbers[None, None, :]).astype(jnp.int32)
    per_token = jnp.sum(onehot, axis=1)
    before = jnp.cumsum(per_token, axis=0) - per_token
    return jnp.sum(onehot * before[:, None, :], axis=2)


def row_positions(routes, experts_here, groups, capacity):
    slot_index = slot_numbers(routes, experts_here * groups)
    holder = routes // experts_here
    within = routes - holder * experts_here
    return ((within * groups + holder) * capacity + slot_index).reshape(-1)


def place_rows(gates, values, positions, total_rows):
    scaled = (gates[:, :, None] * values[:, None, :].astype(jnp.float32)).astype(jnp.bfloat16)
    outgoing = jnp.zeros((total_rows, values.shape[1]), jnp.bfloat16)
    return outgoing.at[positions].set(scaled.reshape(-1, values.shape[1]))


def unfused(
    forward_routes,
    forward_gates,
    hidden_rows,
    down_weight,
    shared_hidden,
    shared_weight,
    backward_routes,
    backward_gates,
    cotangent,
):
    experts_here = down_weight.shape[1]
    features = down_weight.shape[3]
    capacity = hidden_rows.shape[3]
    groups = lax.axis_size("expert")
    token_count = forward_routes.shape[1]
    top_count = forward_routes.shape[2]
    hidden = hidden_rows[0]
    weight = down_weight[0]
    local_shared = shared_hidden[0]
    shared_piece = shared_weight[0]
    shared_part = jnp.dot(
        local_shared,
        lax.all_gather(shared_piece, "expert", axis=1, tiled=True),
        preferred_element_type=jnp.float32,
    )
    fore_positions = row_positions(forward_routes[0], experts_here, groups, capacity)
    fore_gates = forward_gates[0]
    partial_value = jnp.einsum(
        "egmh,ehd->egmd", hidden, weight, preferred_element_type=jnp.float32
    ).astype(jnp.bfloat16)
    arrived = lax.all_to_all(partial_value, "expert", split_axis=1, concat_axis=1, tiled=True)
    picked = arrived.reshape(-1, features)[fore_positions].reshape(token_count, top_count, features)
    summand = shared_part + jnp.sum(picked.astype(jnp.float32) * fore_gates[:, :, None], axis=1)
    summed = lax.psum_scatter(summand, "tensor", scatter_dimension=1, tiled=True)
    layer_out = summed.astype(jnp.bfloat16)
    handed = shifted(layer_out, "phase", 1)
    cotangent_whole = lax.all_gather(cotangent[0], "tensor", axis=1, tiled=True)
    back_positions = row_positions(backward_routes[0], experts_here, groups, capacity)
    total_rows = experts_here * groups * capacity
    outgoing = place_rows(backward_gates[0], cotangent_whole, back_positions, total_rows)
    received = lax.all_to_all(
        outgoing.reshape(experts_here, groups, capacity, features),
        "expert",
        split_axis=1,
        concat_axis=1,
        tiled=True,
    )
    hidden_back = jnp.einsum(
        "egmd,ehd->egmh", received, weight, preferred_element_type=jnp.float32
    ).astype(jnp.bfloat16)
    shared_back = lax.dot_general(
        cotangent_whole,
        lax.all_gather(shared_piece, "expert", axis=1, tiled=True),
        (((1,), (1,)), ((), ())),
        preferred_element_type=jnp.float32,
    )
    return (handed[None], hidden_back[None], shared_back.astype(jnp.bfloat16)[None])


def solution(mesh):
    sizes = tuple(mesh.shape[axis] for axis in ("phase", "expert", "tensor"))

    def on_device(*arrays):
        phases, ne, nt = sizes
        hidden, weight, cot = arrays[2], arrays[3], arrays[8]
        two_chips = ne == 4 and ne == nt and phases > 1
        fits = 2 * arrays[0].shape[1] <= LANES and cot.shape[2] % LANES == 0
        if two_chips and fits:
            return fused(sizes, *arrays)
        return unfused(*arrays)

    return jax.shard_map(
        on_device,
        mesh=mesh,
        in_specs=(
            P("phase", "expert", None),
            P("phase", "expert", None),
            P("phase", "expert", None, None, "tensor"),
            P("phase", "expert", "tensor", None),
            P("phase", "expert", "tensor"),
            P("phase", "tensor", "expert"),
            P("phase", "expert", None),
            P("phase", "expert", None),
            P("phase", "expert", "tensor"),
        ),
        out_specs=(
            P("phase", "expert", "tensor"),
            P("phase", "expert", None, None, "tensor"),
            P("phase", "expert", "tensor"),
        ),
        check_vma=False,
    )
```

time: 48 us -> 46.2 us (0.963)
  Pallas kernels: 35.9 us -> 34.6 us
  local copies, waits for them, and re-layouts: 11 us -> 10.4 us
    pallas_call x1 -> x2, Pallas kernels: 35.9 us -> 34.6 us  [the longest x1 32.9 us: fused(): pl.pallas_call(functools.partial(fused_kernel, sizes), out_shape=results,...]
    unnamed x16 -> x24, local copies, waits for them, and re-layouts: 11 us -> 10.4 us
where the time goes in v2:
time: 46.2 us; the launch traced here: 45.7 us
  Pallas kernels  34.6 us (75%)
  local copies, waits for them, and re-layouts  10.4 us (23%)
  between operations  0.67 us (1%)
    pallas_call x1, Pallas kernels, fused(): pl.pallas_call(functools.partial(fused_kernel, sizes), out_shape=results,...  32.9 us
    unnamed x24, local copies, waits for them, and re-layouts  10.4 us
    pallas_call x1, Pallas kernels, fused(): pl.pallas_call(store_kernel, out_shape=results, in_specs=[vmem] * 3, out_...  1.73 us

profile of v2, /device:TPU:0, one launch (start us, length us, event | category | flops | bytes accessed | tf_op | source)
XLA Modules:
  0.0 45.7 jit_solution(8263990555490551595)
XLA Ops:
  0.6 0.0 copy-start
  0.6 2.1 %copy-done = bf16[1,3,256,2560]{3,2,1,0:T(8,128)(2,1)S(1)} copy-done((bf16[1,3,256,2560]{3,2,1,0:T(8,128)(2,1)S(1)}, bf16[1,3,256,2560]{3,2,1,0:T(8,128)(2,1)}, u32[]{:S(2)}) %copy-start) | copy-done | bytes 3932184
  2.7 0.0 copy-start.1
  2.8 1.0 %copy-done.1 = bf16[1,384,640]{2,1,0:T(8,128)(2,1)S(1)} copy-done((bf16[1,384,640]{2,1,0:T(8,128)(2,1)S(1)}, bf16[1,384,640]{2,1,0:T(8,128)(2,1)}, u32[]{:S(2)}) %copy-start.1) | copy-done | bytes 491544
  3.8 0.0 copy-start.2
  3.8 0.9 %copy-done.2 = bf16[1,3,4,43,256]{4,2,3,1,0:T(4,128)(2,1)S(1)} copy-done((bf16[1,3,4,43,256]{4,2,3,1,0:T(4,128)(2,1)S(1)}, bf16[1,3,4,43,256]{4,2,3,1,0:T(4,128)(2,1)}, u32[]{:S(2)}) %copy-start.2) | copy-done | bytes 264216
  4.7 0.0 copy-start.5
  4.7 0.9 %copy-done.5 = bf16[1,64,640]{2,1,0:T(8,128)(2,1)S(1)} copy-done((bf16[1,64,640]{2,1,0:T(8,128)(2,1)S(1)}, bf16[1,64,640]{2,1,0:T(8,128)(2,1)}, u32[]{:S(2)}) %copy-start.5) | copy-done | bytes 81944
  5.6 0.0 copy-start.6
  5.6 0.8 %copy-done.6 = bf16[1,64,384]{2,1,0:T(8,128)(2,1)S(1)} copy-done((bf16[1,64,384]{2,1,0:T(8,128)(2,1)S(1)}, bf16[1,64,384]{2,1,0:T(8,128)(2,1)}, u32[]{:S(2)}) %copy-start.6) | copy-done | bytes 49176
  6.4 0.0 copy-start.8
  6.4 0.7 %copy-done.8 = s32[1,64,6]{1,0,2:T(1,128)S(1)} copy-done((s32[1,64,6]{1,0,2:T(1,128)S(1)}, s32[1,64,6]{1,0,2:T(1,128)}, u32[]{:S(2)}) %copy-start.8) | copy-done | bytes 1560
  7.1 0.0 copy-start.9
  7.1 0.7 %copy-done.9 = f32[1,64,6]{1,0,2:T(1,128)S(1)} copy-done((f32[1,64,6]{1,0,2:T(1,128)S(1)}, f32[1,64,6]{1,0,2:T(1,128)}, u32[]{:S(2)}) %copy-start.9) | copy-done | bytes 1560
  7.8 0.0 copy-start.10
  7.8 0.7 %copy-done.10 = s32[1,64,6]{1,0,2:T(1,128)S(1)} copy-done((s32[1,64,6]{1,0,2:T(1,128)S(1)}, s32[1,64,6]{1,0,2:T(1,128)}, u32[]{:S(2)}) %copy-start.10) | copy-done | bytes 1560
  8.5 0.0 copy-start.11
  8.5 0.7 %copy-done.11 = f32[1,64,6]{1,0,2:T(1,128)S(1)} copy-done((f32[1,64,6]{1,0,2:T(1,128)S(1)}, f32[1,64,6]{1,0,2:T(1,128)}, u32[]{:S(2)}) %copy-start.11) | copy-done | bytes 1560
  9.2 32.9 %shard_map.112 = (bf16[64,640]{1,0:T(8,128)(2,1)S(1)}, bf16[3,43,4,256]{3,2,1,0:T(4,128)(2,1)S(1)}, bf16[64,384]{1,0:T(8,128)(2,1)S(1)}) custom-call(s32[6,1,64]{2,1,0:T(1,128)S(1)} %bitcast.21, f32[6,1,64]{2,1,0:T(1,128)S(1)} %bitcast.22, s32[6,1,64]{2,1,0:T(1,128)S(1)} %bitcast.23, f32[6,1,64]{2,1,0:T(1,128)S(1)} %bitcast.24, ...), custom_call_target="tpu_custom_call" | custom-call | tf_op jit(solution)/shard_map/pallas_call | solution.py:263
  42.1 0.0 copy-start.3
  42.1 0.7 %copy-done.3 = bf16[3,43,4,256]{3,2,1,0:T(4,128)(2,1)} copy-done((bf16[3,43,4,256]{3,2,1,0:T(4,128)(2,1)}, bf16[3,43,4,256]{3,2,1,0:T(4,128)(2,1)S(1)}, u32[]{:S(2)}) %copy-start.3) | copy-done | bytes 264216
  42.8 0.0 copy-start.4
  42.8 0.6 %copy-done.4 = bf16[64,640]{1,0:T(8,128)(2,1)} copy-done((bf16[64,640]{1,0:T(8,128)(2,1)}, bf16[64,640]{1,0:T(8,128)(2,1)S(1)}, u32[]{:S(2)}) %copy-start.4) | copy-done | bytes 81944
  43.4 0.0 copy-start.7
  43.4 0.6 %copy-done.7 = bf16[64,384]{1,0:T(8,128)(2,1)} copy-done((bf16[64,384]{1,0:T(8,128)(2,1)}, bf16[64,384]{1,0:T(8,128)(2,1)S(1)}, u32[]{:S(2)}) %copy-start.7) | copy-done | bytes 49176
  44.0 1.7 %shard_map.113 = (bf16[64,640]{1,0:T(8,128)(2,1)}, bf16[3,43,4,256]{3,2,1,0:T(4,128)(2,1)}, bf16[64,384]{1,0:T(8,128)(2,1)}) custom-call(bf16[64,640]{1,0:T(8,128)(2,1)} %copy-done.4, bf16[3,43,4,256]{3,2,1,0:T(4,128)(2,1)} %copy-done.3, bf16[64,384]{1,0:T(8,128)(2,1)} %copy-done.7), custom_call_target="tpu_custom_call" | custom-call | tf_op jit(solution)/shard_map/pallas_call | solution.py:307
Async XLA Ops:
  0.6 2.1 %copy-start = (bf16[1,3,256,2560]{3,2,1,0:T(8,128)(2,1)S(1)}, bf16[1,3,256,2560]{3,2,1,0:T(8,128)(2,1)}, u32[]{:S(2)}) copy-start(bf16[1,3,256,2560]{3,2,1,0:T(8,128)(2,1)} %param.12) | copy-start | bytes 11796484
  2.7 1.0 %copy-start.1 = (bf16[1,384,640]{2,1,0:T(8,128)(2,1)S(1)}, bf16[1,384,640]{2,1,0:T(8,128)(2,1)}, u32[]{:S(2)}) copy-start(bf16[1,384,640]{2,1,0:T(8,128)(2,1)} %param.14) | copy-start | bytes 1474564
  3.8 1.0 %copy-start.2 = (bf16[1,3,4,43,256]{4,2,3,1,0:T(4,128)(2,1)S(1)}, bf16[1,3,4,43,256]{4,2,3,1,0:T(4,128)(2,1)}, u32[]{:S(2)}) copy-start(bf16[1,3,4,43,256]{4,2,3,1,0:T(4,128)(2,1)} %param.11) | copy-start | bytes 792580
  4.7 0.9 %copy-start.5 = (bf16[1,64,640]{2,1,0:T(8,128)(2,1)S(1)}, bf16[1,64,640]{2,1,0:T(8,128)(2,1)}, u32[]{:S(2)}) copy-start(bf16[1,64,640]{2,1,0:T(8,128)(2,1)} %param.17) | copy-start | bytes 245764
  5.6 0.8 %copy-start.6 = (bf16[1,64,384]{2,1,0:T(8,128)(2,1)S(1)}, bf16[1,64,384]{2,1,0:T(8,128)(2,1)}, u32[]{:S(2)}) copy-start(bf16[1,64,384]{2,1,0:T(8,128)(2,1)} %param.13) | copy-start | bytes 147460
  6.4 0.7 %copy-start.8 = (s32[1,64,6]{1,0,2:T(1,128)S(1)}, s32[1,64,6]{1,0,2:T(1,128)}, u32[]{:S(2)}) copy-start(s32[1,64,6]{1,0,2:T(1,128)} %param.9) | copy-start | bytes 4612
  7.1 0.7 %copy-start.9 = (f32[1,64,6]{1,0,2:T(1,128)S(1)}, f32[1,64,6]{1,0,2:T(1,128)}, u32[]{:S(2)}) copy-start(f32[1,64,6]{1,0,2:T(1,128)} %param.10) | copy-start | bytes 4612
  7.8 0.7 %copy-start.10 = (s32[1,64,6]{1,0,2:T(1,128)S(1)}, s32[1,64,6]{1,0,2:T(1,128)}, u32[]{:S(2)}) copy-start(s32[1,64,6]{1,0,2:T(1,128)} %param.15) | copy-start | bytes 4612
  8.5 0.7 %copy-start.11 = (f32[1,64,6]{1,0,2:T(1,128)S(1)}, f32[1,64,6]{1,0,2:T(1,128)}, u32[]{:S(2)}) copy-start(f32[1,64,6]{1,0,2:T(1,128)} %param.16) | copy-start | bytes 4612
  42.1 0.7 %copy-start.3 = (bf16[3,43,4,256]{3,2,1,0:T(4,128)(2,1)}, bf16[3,43,4,256]{3,2,1,0:T(4,128)(2,1)S(1)}, u32[]{:S(2)}) copy-start(bf16[3,43,4,256]{3,2,1,0:T(4,128)(2,1)S(1)} %get-tuple-element.10.refs_1_) | copy-start | bytes 792580
  42.8 0.6 %copy-start.4 = (bf16[64,640]{1,0:T(8,128)(2,1)}, bf16[64,640]{1,0:T(8,128)(2,1)S(1)}, u32[]{:S(2)}) copy-start(bf16[64,640]{1,0:T(8,128)(2,1)S(1)} %get-tuple-element.9.refs_0_) | copy-start | bytes 245764
  43.4 0.6 %copy-start.7 = (bf16[64,384]{1,0:T(8,128)(2,1)}, bf16[64,384]{1,0:T(8,128)(2,1)S(1)}, u32[]{:S(2)}) copy-start(bf16[64,384]{1,0:T(8,128)(2,1)S(1)} %get-tuple-element.11.refs_2_) | copy-start | bytes 147460

commit v3 on v2

--- a/solution.py
+++ b/solution.py
@@ -299,10 +299,15 @@
             collective_id=0, has_side_effects=True, vmem_limit_bytes=32 * 1024 * 1024
         ),
     )(
-        *(a.transpose(2, 0, 1) for a in (fr, fg, br, bg)),
-        hidden[0].transpose(0, 2, 1, 3),
-        weight.reshape(here * hq, features),
-        shared[0], sweight[0], cot[0],
+        *(
+            pltpu.with_memory_space_constraint(a, pltpu.HBM)
+            for a in (
+                *(r.transpose(2, 0, 1) for r in (fr, fg, br, bg)),
+                hidden[0].transpose(0, 2, 1, 3),
+                weight.reshape(here * hq, features),
+                shared[0], sweight[0], cot[0],
+            )
+        )
     )
     handed, hgrad, sgrad = pl.pallas_call(
         store_kernel,
@@ -310,6 +315,7 @@
         in_specs=[vmem] * 3,
         out_specs=[hbm] * 3,
         scratch_shapes=[pltpu.SemaphoreType.DMA((3,))],
+        compiler_params=pltpu.CompilerParams(vmem_limit_bytes=4 * 1024 * 1024),
     )(*made)
     return handed[None], hgrad.transpose(0, 2, 1, 3)[None], sgrad[None]
 

time: 46.2 us -> 33.8 us (0.73)
  local copies, waits for them, and re-layouts: 10.4 us -> 0 us
  Pallas kernels: 34.6 us -> 33 us
    unnamed x24 -> x0, local copies, waits for them, and re-layouts: 10.4 us -> none
    pallas_call x1, Pallas kernels: 1.73 us -> 0.76 us  [fused(): pl.pallas_call(store_kernel, out_shape=results, in_specs=[vmem] * 3, out_...]
    pallas_call x1, Pallas kernels: 32.9 us -> 32.2 us  [fused(): pl.pallas_call(functools.partial(fused_kernel, sizes), out_shape=results,...]
where the time goes in v3:
time: 33.8 us; the launch traced here: 33.6 us
  Pallas kernels  33 us (98%)
  between operations  0.64 us (2%)
    pallas_call x1, Pallas kernels, fused(): pl.pallas_call(functools.partial(fused_kernel, sizes), out_shape=results,...  32.2 us
    pallas_call x1, Pallas kernels, fused(): pl.pallas_call(store_kernel, out_shape=results, in_specs=[vmem] * 3, out_...  0.76 us

profile of v3, /device:TPU:0, one launch (start us, length us, event | category | flops | bytes accessed | tf_op | source)
XLA Modules:
  0.0 33.6 jit_solution(12178994184530926336)
XLA Ops:
  0.6 32.2 %shard_map.112 = (bf16[64,640]{1,0:T(8,128)(2,1)S(1)}, bf16[3,43,4,256]{3,2,1,0:T(4,128)(2,1)S(1)}, bf16[64,384]{1,0:T(8,128)(2,1)S(1)}) custom-call(s32[6,1,64]{2,1,0:T(1,128)} %bitcast.21, f32[6,1,64]{2,1,0:T(1,128)} %bitcast.22, s32[6,1,64]{2,1,0:T(1,128)} %bitcast.23, f32[6,1,64]{2,1,0:T(1,128)} %bitcast.24, bf16[3,43,4,256]{3,2,1,0:T(4,128)(2,1)} %bitcast.18, ...), custom_call_target="tpu_custom_call" | custom-call | tf_op jit(solution)/shard_map/pallas_call | solution.py:263
  32.8 0.8 %shard_map.113 = (bf16[64,640]{1,0:T(8,128)(2,1)}, bf16[3,43,4,256]{3,2,1,0:T(4,128)(2,1)}, bf16[64,384]{1,0:T(8,128)(2,1)}) custom-call(bf16[64,640]{1,0:T(8,128)(2,1)S(1)} %get-tuple-element.9.refs_0_, bf16[3,43,4,256]{3,2,1,0:T(4,128)(2,1)S(1)} %get-tuple-element.10.refs_1_, bf16[64,384]{1,0:T(8,128)(2,1)S(1)} %get-tuple-element.11.refs_2_), custom_call_target="tpu_custom_call" | custom-call | tf_op jit(solution)/shard_map/pallas_call | solution.py:312

commit v4 on v3

--- a/solution.py
+++ b/solution.py
@@ -56,6 +56,33 @@
     for partner in partners:
         pl.semaphore_signal(barrier, inc=1, device_id=partner, device_id_type=MESH)
 
+    copies = []
+
+    def send(src, dst, to):
+        i = len(copies)
+        copy = pltpu.make_async_remote_copy(
+            src_ref=src, dst_ref=dst, send_sem=send_sem.at[i], recv_sem=recv_sem.at[i],
+            device_id=to, device_id_type=MESH,
+        )
+        copy.start()
+        copies.append(copy)
+        return copy
+
+    def spread(buffer):
+        return [send(buffer.at[e], buffer.at[e], {"expert": o}) for o in (far, sib)]
+
+    def hand_on(buffer, pair):
+        pair[0].wait_recv()
+        pair.append(send(buffer.at[far], buffer.at[far], {"expert": sib}))
+
+    pl.semaphore_wait(barrier, len(partners))
+    loads[4].wait()
+    mine = cot.at[z, e]
+    z_copies = [send(mine, mine, {"tensor": o}) for o in others_t]
+    loads[5].wait()
+    sh_copies = spread(sh)
+    y_copies, sib_copies, far_copies = [], [], []
+
     for load in loads[:4]:
         load.wait()
     across = 2 * experts
@@ -75,36 +102,11 @@
     )
     pack[e] = jnp.where(level < experts, jnp.where(hot > 0.5, counts, -1.0), gate)
 
-    copies = []
-
-    def send(src, dst, to):
-        i = len(copies)
-        copy = pltpu.make_async_remote_copy(
-            src_ref=src, dst_ref=dst, send_sem=send_sem.at[i], recv_sem=recv_sem.at[i],
-            device_id=to, device_id_type=MESH,
-        )
-        copy.start()
-        copies.append(copy)
-        return copy
-
-    def spread(buffer):
-        return [send(buffer.at[e], buffer.at[e], {"expert": o}) for o in (far, sib)]
-
-    def hand_on(buffer, pair):
-        pair[0].wait_recv()
-        pair.append(send(buffer.at[far], buffer.at[far], {"expert": sib}))
-
-    pl.semaphore_wait(barrier, len(partners))
     pack_copies = spread(pack)
-    loads[5].wait()
-    sh_copies = spread(sh)
-    loads[4].wait()
-    mine = cot.at[z, e]
-    z_copies = [send(mine, mine, {"tensor": o}) for o in others_t]
-    y_copies = [send(mine, mine, {"expert": far})]
-    sib_copies = [send(mine, mine, {"expert": sib})]
+    y_copies.append(send(mine, mine, {"expert": far}))
+    sib_copies.append(send(mine, mine, {"expert": sib}))
+    hand_on(sh, sh_copies)
     hand_on(pack, pack_copies)
-    hand_on(sh, sh_copies)
 
     order = (far_sib, sib, far, e)
     level = lax.broadcasted_iota(jnp.int32, (tok, across), 1)
@@ -155,21 +157,19 @@
         s1.append(send(s1_out.at[s], s1_in.at[s], {"expert": sib}))
         for g in range(2):
             keep[s, g] = acc[(2 + g) * tok:(3 + g) * tok, :]
-        if 1 <= s < nt - 1:
-            relay(s + 1)
-    for s in range(nt):
+
+    def reduce_core(s):
         s1[s].wait_recv()
         s2_out[s] = (keep[s, 0] + s1_in[s, 0].astype(F32)).astype(BF16)
         s2.append(send(s2_out.at[s], s2_in.at[s], {"expert": far}))
         keep[s, 1] = keep[s, 1] + s1_in[s, 1].astype(F32)
 
-    far_copies = []
-    for d in range(nt):
+    def hand_over(d):
         y_copies[d].wait_recv()
         piece = cot.at[lax.rem(z + nt - d, nt), far]
         far_copies.append(send(piece, piece, {"expert": sib}))
 
-    for d in range(nt):
+    def back_part(d):
         f = lax.rem(z + nt - d, nt)
         sib_copies[d].wait_recv()
         far_copies[d].wait_recv()
@@ -183,14 +183,6 @@
         else:
             back[...] += part
 
-    sg_part[...] = lax.dot_general(
-        cot[e].reshape(ne * tok, dt), sw[...], (((1,), (1,)), ((), ())),
-        preferred_element_type=F32,
-    ).reshape(ne, tok, hs)
-    for g in range(2):
-        sg_out[g] = sg_part[order[g]].astype(BF16)
-    sg = send(sg_out, sg_in, {"expert": sib})
-
     def reduce_z(s):
         s2[s].wait_recv()
         s3_out[s] = (keep[s, 1] + s2_in[s].astype(F32)).astype(BF16)
@@ -209,16 +201,39 @@
             cap, ne, hq
         )
 
-    reduce_z(0)
+    half = nt // 2
+    for s in range(half):
+        reduce_core(s)
+    for d in range(half):
+        hand_over(d)
+    for d in range(2, nt):
+        relay(d)
+    for s in range(half, nt):
+        reduce_core(s)
+    for d in range(half):
+        back_part(d)
+    for s in range(half):
+        reduce_z(s)
+    for d in range(half, nt):
+        hand_over(d)
+    for d in range(half, nt):
+        back_part(d)
+
+    sg_part[...] = lax.dot_general(
+        cot[e].reshape(ne * tok, dt), sw[...], (((1,), (1,)), ((), ())),
+        preferred_element_type=F32,
+    ).reshape(ne, tok, hs)
+    for g in range(2):
+        sg_out[g] = sg_part[order[g]].astype(BF16)
+    sg = send(sg_out, sg_in, {"expert": sib})
     rows_back(0)
     sg.wait_recv()
     sg_out2[...] = (sg_part[far] + sg_in[0].astype(F32)).astype(BF16)
     sg2 = send(sg_out2, sg_in2, {"expert": far})
-    reduce_z(1)
+    for s in range(half, nt):
+        reduce_z(s)
     for i in range(1, here):
         rows_back(i)
-    for s in range(2, nt):
-        reduce_z(s)
     sg2.wait_recv()
     sgrad_ref[...] = (
         sg_part[e] + sg_in[1].astype(F32) + sg_in2[...].astype(F32)

time: 33.8 us -> 33.2 us (0.982)
  Pallas kernels: 33 us -> 32.4 us
    pallas_call x1, Pallas kernels: 32.2 us -> 31.6 us  [fused(): pl.pallas_call(functools.partial(fused_kernel, sizes), out_shape=results,...]
where the time goes in v4:
time: 33.2 us; the launch traced here: 33 us
  Pallas kernels  32.4 us (98%)
  between operations  0.64 us (2%)
    pallas_call x1, Pallas kernels, fused(): pl.pallas_call(functools.partial(fused_kernel, sizes), out_shape=results,...  31.6 us
    pallas_call x1, Pallas kernels, fused(): pl.pallas_call(store_kernel, out_shape=results, in_specs=[vmem] * 3, out_...  0.76 us

profile of v4, /device:TPU:0, one launch (start us, length us, event | category | flops | bytes accessed | tf_op | source)
XLA Modules:
  0.0 33.0 jit_solution(12209315311719562036)
XLA Ops:
  0.6 31.6 %shard_map.112 = (bf16[64,640]{1,0:T(8,128)(2,1)S(1)}, bf16[3,43,4,256]{3,2,1,0:T(4,128)(2,1)S(1)}, bf16[64,384]{1,0:T(8,128)(2,1)S(1)}) custom-call(s32[6,1,64]{2,1,0:T(1,128)} %bitcast.21, f32[6,1,64]{2,1,0:T(1,128)} %bitcast.22, s32[6,1,64]{2,1,0:T(1,128)} %bitcast.23, f32[6,1,64]{2,1,0:T(1,128)} %bitcast.24, bf16[3,43,4,256]{3,2,1,0:T(4,128)(2,1)} %bitcast.18, ...), custom_call_target="tpu_custom_call" | custom-call | tf_op jit(solution)/shard_map/pallas_call | solution.py:278
  32.3 0.8 %shard_map.113 = (bf16[64,640]{1,0:T(8,128)(2,1)}, bf16[3,43,4,256]{3,2,1,0:T(4,128)(2,1)}, bf16[64,384]{1,0:T(8,128)(2,1)}) custom-call(bf16[64,640]{1,0:T(8,128)(2,1)S(1)} %get-tuple-element.9.refs_0_, bf16[3,43,4,256]{3,2,1,0:T(4,128)(2,1)S(1)} %get-tuple-element.10.refs_1_, bf16[64,384]{1,0:T(8,128)(2,1)S(1)} %get-tuple-element.11.refs_2_), custom_call_target="tpu_custom_call" | custom-call | tf_op jit(solution)/shard_map/pallas_call | solution.py:327

commit v5 on v4

--- a/solution.py
+++ b/solution.py
@@ -136,7 +136,13 @@
         y_copies.append(send(piece, piece, {"expert": far}))
         sib_copies.append(send(piece, piece, {"expert": sib}))
 
+    def hand_over(d):
+        y_copies[d].wait_recv()
+        piece = cot.at[lax.rem(z + nt - d, nt), far]
+        far_copies.append(send(piece, piece, {"expert": sib}))
+
     relay(1)
+    hand_over(0)
     loads[7].wait()
     loads[8].wait()
     sh_copies[1].wait_recv()
@@ -163,11 +169,6 @@
         s2_out[s] = (keep[s, 0] + s1_in[s, 0].astype(F32)).astype(BF16)
         s2.append(send(s2_out.at[s], s2_in.at[s], {"expert": far}))
         keep[s, 1] = keep[s, 1] + s1_in[s, 1].astype(F32)
-
-    def hand_over(d):
-        y_copies[d].wait_recv()
-        piece = cot.at[lax.rem(z + nt - d, nt), far]
-        far_copies.append(send(piece, piece, {"expert": sib}))
 
     def back_part(d):
         f = lax.rem(z + nt - d, nt)
@@ -202,12 +203,13 @@
         )
 
     half = nt // 2
+    for d in range(2, nt - 1):
+        relay(d)
     for s in range(half):
         reduce_core(s)
-    for d in range(half):
+    relay(nt - 1)
+    for d in range(1, half):
         hand_over(d)
-    for d in range(2, nt):
-        relay(d)
     for s in range(half, nt):
         reduce_core(s)
     for d in range(half):

time: 33.2 us -> 33.2 us (level)
  no operation moved by 1% of the time
where the time goes in v5:
time: 33.2 us; the launch traced here: 33 us
  Pallas kernels  32.4 us (98%)
  between operations  0.64 us (2%)
    pallas_call x1, Pallas kernels, fused(): pl.pallas_call(functools.partial(fused_kernel, sizes), out_shape=results,...  31.6 us
    pallas_call x1, Pallas kernels, fused(): pl.pallas_call(store_kernel, out_shape=results, in_specs=[vmem] * 3, out_...  0.76 us

profile of v5, /device:TPU:0, one launch (start us, length us, event | category | flops | bytes accessed | tf_op | source)
XLA Modules:
  0.0 33.0 jit_solution(15624119972276703978)
XLA Ops:
  0.6 31.6 %shard_map.112 = (bf16[64,640]{1,0:T(8,128)(2,1)S(1)}, bf16[3,43,4,256]{3,2,1,0:T(4,128)(2,1)S(1)}, bf16[64,384]{1,0:T(8,128)(2,1)S(1)}) custom-call(s32[6,1,64]{2,1,0:T(1,128)} %bitcast.21, f32[6,1,64]{2,1,0:T(1,128)} %bitcast.22, s32[6,1,64]{2,1,0:T(1,128)} %bitcast.23, f32[6,1,64]{2,1,0:T(1,128)} %bitcast.24, bf16[3,43,4,256]{3,2,1,0:T(4,128)(2,1)} %bitcast.18, ...), custom_call_target="tpu_custom_call" | custom-call | tf_op jit(solution)/shard_map/pallas_call | solution.py:280
  32.3 0.8 %shard_map.113 = (bf16[64,640]{1,0:T(8,128)(2,1)}, bf16[3,43,4,256]{3,2,1,0:T(4,128)(2,1)}, bf16[64,384]{1,0:T(8,128)(2,1)}) custom-call(bf16[64,640]{1,0:T(8,128)(2,1)S(1)} %get-tuple-element.9.refs_0_, bf16[3,43,4,256]{3,2,1,0:T(4,128)(2,1)S(1)} %get-tuple-element.10.refs_1_, bf16[64,384]{1,0:T(8,128)(2,1)S(1)} %get-tuple-element.11.refs_2_), custom_call_target="tpu_custom_call" | custom-call | tf_op jit(solution)/shard_map/pallas_call | solution.py:329
